TPU v7x, 32 devices: a whole 2x2x4 slice. The times are simulated.
32 devices in a mesh: half: 1, grp: 4 (over y, core), dev: 8 (over z, x).
Axes of the slice: x: 2, y: 2, z: 4, core: 2. Of those that a mesh axis runs over, the one named last changes fastest.
Arguments:
- panel_block: float32 [2048, 512], P(('half', 'grp', 'dev')), may hold values from -1 to 1, as said below
- trailing: float32 [2048, 1024], P(('half', 'grp'), 'dev'), may hold values from -6 to 6
Outputs:
- triangle: float32 [512, 512], replicated
- projected: float32 [512, 1024], P(None, 'dev')
- remainder: float32 [2048, 1024], P(('half', 'grp'), 'dev')
Inputs may be any that keep to these rules, and one draw needn't show every extreme that they name: `panel_block`: of full column rank.
All inputs are finite; a program needn't handle non-finite values.
Results may differ from a plain program's by a relative error of at most 0.0003.
Values sent between devices are 32-bit elements; how exact they have to be, the bound alone decides.
A program may use at most 64 MiB of HBM per device.

v0:
```python
import jax
import jax.numpy as jnp
from jax import lax
from jax.sharding import PartitionSpec as P


def on_device(panel_block, trailing):
    highest = lax.Precision.HIGHEST
    panel_group = lax.all_gather(panel_block, "dev", axis=0, tiled=True)
    gram_part = jnp.dot(panel_group.T, panel_group, precision=highest)
    cross_part = jnp.dot(panel_group.T, trailing, precision=highest)
    gram_sum, cross_sum = lax.psum((gram_part, cross_part), ("half", "grp"))
    factor = jnp.linalg.cholesky(gram_sum)
    projected = lax.linalg.triangular_solve(factor, cross_sum, left_side=True, lower=True)
    solved = lax.linalg.triangular_solve(
        factor, projected, left_side=True, lower=True, transpose_a=True
    )
    remainder = trailing - jnp.dot(panel_group, solved, precision=highest)
    triangle = factor.T
    return (triangle, projected, remainder)


def solution(mesh):
    placed = (P(("half", "grp", "dev"), None), P(("half", "grp"), "dev"))
    return jax.shard_map(
        on_device,
        mesh=mesh,
        in_specs=placed,
        out_specs=(P(), P(None, "dev"), P(("half", "grp"), "dev")),
        check_vma=False,
    )
```

profile of v0, /device:TPU:0, one launch (start us, length us, event | category | flops | bytes accessed | tf_op | source)
XLA Modules:
  0.0 260.0 jit_solution(11239562665385252636)
XLA Ops:
  7.2 0.7 all-gather.2.cloned.1.call-update
  8.0 45.2 %all-gather.2.cloned.1.call-done = f32[512,512]{1,0:T(8,128)} async-done(((f32[64,512]{1,0:T(8,128)}), f32[512,512]{1,0:T(8,128)}) %all-gather.2.cloned.1.call-update) | async-done | bytes 1048592 | tf_op jit(solution)/shard_map/all_gather | solution.py:9
  53.1 4.5 %fusion.59 = f32[512,512]{0,1:T(8,128)} fusion(f32[512,512]{1,0:T(8,128)} %all-gather.2.cloned.1.call-done), kind=kOutput, calls=%fused_computation.99 | convolution fusion | flops 1610612736 | bytes 2097152 | tf_op jit(solution)/shard_map/dot_general | solution.py:10
  57.6 2.5 fusion.60
  60.3 37.8 %all-reduce.4.cloned.1.call-done = (f32[512,512]{0,1:T(8,128)}, f32[512,128]{1,0:T(8,128)}) async-done(((f32[512,512]{0,1:T(8,128)}, f32[512,128]{1,0:T(8,128)}), (f32[512,512]{0,1:T(8,128)}, f32[512,128]{1,0:T(8,128)})) %all-reduce.4.cloned.1.call-update) | async-done | bytes 1310736 | tf_op jit(solution)/shard_map/psum | solution.py:12
  98.2 1.6 copy.6
  100.1 1.0 copy-done.3
  101.0 11.7 %cholesky.104 = f32[128,128]{1,0:T(8,128)S(1)} custom-call(f32[128,128]{1,0:T(8,128)S(1)} %cholesky.266), custom_call_target="Cholesky" | custom-call | tf_op jit(solution)/shard_map/jit(cholesky)/cholesky | solution.py:13
  112.8 9.8 %custom-call.32 = f32[1,128,128]{1,2,0:T(8,128)S(1)} custom-call(f32[1,128,128]{2,1,0:T(8,128)S(1)} %get-tuple-element.37), custom_call_target="InvertDiagBlocksLowerTriangular" | custom-call | tf_op jit(solution)/shard_map/jit(cholesky)/cholesky | solution.py:13
  122.7 0.3 constant_dynamic-update-slice_fusion.3
  123.1 0.3 convolution_subtract_fusion
  123.4 0.7 copy-done.6
  124.1 11.9 %cholesky.217 = f32[128,128]{1,0:T(8,128)S(1)} custom-call(f32[128,128]{1,0:T(8,128)S(1)} %cholesky.270), custom_call_target="Cholesky" | custom-call | tf_op jit(solution)/shard_map/jit(cholesky)/cholesky | solution.py:13
  136.0 9.8 %custom-call.33 = f32[1,128,128]{1,2,0:T(8,128)S(1)} custom-call(f32[1,128,128]{2,1,0:T(8,128)S(1)} %get-tuple-element.34), custom_call_target="InvertDiagBlocksLowerTriangular" | custom-call | tf_op jit(solution)/shard_map/jit(cholesky)/cholesky | solution.py:13
  145.8 1.2 convolution_dynamic-update-slice_fusion
  147.0 0.4 convolution_subtract_fusion.1
  147.4 0.6 cholesky.275
  148.0 13.2 %cholesky.238 = f32[128,128]{1,0:T(8,128)} custom-call(f32[128,128]{1,0:T(8,128)} %cholesky.275), custom_call_target="Cholesky" | custom-call | tf_op jit(solution)/shard_map/jit(cholesky)/cholesky | solution.py:13
  161.2 1.5 select_reduce_fusion.1
  162.7 0.7 compare_reduce_fusion.1
  163.4 11.3 %custom-call.34 = f32[1,128,128]{1,2,0:T(8,128)} custom-call(f32[1,128,128]{2,1,0:T(8,128)} %get-tuple-element.31), custom_call_target="InvertDiagBlocksLowerTriangular" | custom-call | tf_op jit(solution)/shard_map/jit(cholesky)/cholesky | solution.py:13
  174.7 1.0 convolution_dynamic-update-slice_fusion.1
  175.7 0.4 convolution_subtract_fusion.8
  176.1 11.9 %cholesky.255 = f32[128,128]{1,0:T(8,128)S(1)} custom-call(f32[128,128]{1,0:T(8,128)S(1)} %convolution_subtract_fusion.8), custom_call_target="Cholesky" | custom-call | tf_op jit(solution)/shard_map/jit(cholesky)/cholesky | solution.py:13
  188.0 0.6 compare_reduce_fusion
  188.6 0.6 compare_reduce_fusion.2
  191.8 1.2 fusion.2
  193.1 10.9 %while.1 = (s32[]{:T(128)}, f32[512,512]{1,0:T(8,128)S(1)}, s32[4,2]{0,1:T(2,128)S(1)}, f32[4,128,128]{2,1,0:T(8,128)}, s32[]{:T(128)}) while((s32[]{:T(128)}, f32[512,512]{1,0:T(8,128)S(1)}, s32[4,2]{0,1:T(2,128)S(1)}, f32[4,128,128]{2,1,0:T(8,128)}, s32[]{:T(128)}) %tuple.33), condition=%wide.while_cond, body=%wide.while_body.sunk | while | flops 2 | bytes 132705 | solution.py:14
  193.1 0.6 fusion.77
  193.7 2.1 bitcast_dynamic-update-slice_fusion.2
  195.9 0.6 fusion.77
  196.5 2.1 bitcast_dynamic-update-slice_fusion.2
  198.6 0.6 fusion.77
  199.2 2.1 bitcast_dynamic-update-slice_fusion.2
  201.3 0.6 fusion.77
  201.9 2.1 bitcast_dynamic-update-slice_fusion.2
  204.0 40.1 %custom-call.35 = f32[4,128,128]{1,2,0:T(8,128)S(1)} custom-call(f32[4,128,128]{2,1,0:T(8,128)} %get-tuple-element.10), custom_call_target="InvertDiagBlocksLowerTriangular" | custom-call | tf_op jit(solution)/shard_map/triangular_solve | solution.py:14
  244.1 1.1 fusion.39
  245.5 0.3 fusion.48
  246.0 0.3 fusion.50
  246.3 0.3 convolution_subtract_fusion.7
  246.7 0.3 fusion.52
  247.2 0.7 pad_maximum_fusion
  248.4 0.4 convolution_subtract_fusion.2
  249.0 0.5 convolution_subtract_fusion.6
  249.7 1.3 fusion
  251.0 0.8 copy.9
  251.8 1.3 copy.8
  (39 shorter events, 2.6 us)
Async XLA Ops:
  7.2 46.0 %all-gather.2.cloned.1.call-start = ((), (), s32[]{:S(2)}) async-start(), calls=%async_computation | async-start | bytes 1179648 | tf_op jit(solution)/shard_map/all_gather | solution.py:9
  7.9 49.7 %copy-start.5 = (f32[512,128]{1,0:T(8,128)S(1)}, f32[512,128]{1,0:T(8,128)}, u32[]{:S(2)}) copy-start(f32[512,128]{1,0:T(8,128)} %param.3) | copy-start | bytes 786436
  7.9 90.2 %all-reduce.4.cloned.1.call-start = ((), (), s32[]{:S(2)}) async-start(), calls=%async_computation.1 | async-start | bytes 2621440 | tf_op jit(solution)/shard_map/psum | solution.py:12
  53.1 4.5 %copy-start = (f32[512,512]{1,0:T(8,128)S(1)}, f32[512,512]{1,0:T(8,128)}, u32[]{:S(2)}) copy-start(f32[512,512]{1,0:T(8,128)} %all-gather.2.cloned.1.call-done) | copy-start | bytes 3145732
  98.2 1.7 copy-start.1
  100.0 1.0 copy-start.3
  101.0 21.7 %copy-start.4 = (f32[512,512]{1,0:T(8,128)S(1)}, f32[512,512]{1,0:T(8,128)}, u32[]{:S(2)}) copy-start(f32[512,512]{1,0:T(8,128)} %copy-done.3) | copy-start | bytes 3145732
  123.4 0.7 copy-start.6
  193.1 52.2 %copy-start.7 = (f32[512,128]{1,0:T(8,128)S(1)}, f32[512,128]{1,0:T(8,128)}, u32[]{:S(2)}) copy-start(f32[512,128]{1,0:T(8,128)} %get-tuple-element.23) | copy-start | bytes 786436
  249.7 2.1 copy-start.2
Sparse Core Ops, SparseCore 0:
  10.1 42.9 all-gather.1
  60.3 37.8 all-reduce.3
where the time goes:
time: 261 us; the launch traced here: 260 us
  other arithmetic  125 us (48%)
  waiting for transfers between devices  83.7 us (32%)
  local copies, waits for them, and re-layouts  17.3 us (7%)
  between operations  16.9 us (6%)
  matrix products  16.6 us (6%)
    another operation x14, other arithmetic, on_device(): factor = jnp.linalg.cholesky(gram_sum)  83.1 us
    all_gather x1, waiting for transfers between devices, on_device(): panel_group = lax.all_gather(panel_block, 'dev', axis=0, tiled=True)  45.2 us
    another operation x4, other arithmetic, on_device(): lax.linalg.triangular_solve(factor, cross_sum, left_side=True, lower=True)  42.1 us
    psum x1, waiting for transfers between devices, on_device(): gram_sum, cross_sum = lax.psum((gram_part, cross_part), ('half', 'grp'))  37.8 us
    another operation x12, local copies, waits for them, and re-layouts  10.9 us
  transfers between devices with their start and end apart: 2, of which 2 were waited for; matrix products, arithmetic and copies ran while one was open for 0% of the time, Pallas kernels for 0%

commit v1 on v0

v1 whole, which is shorter than its diff:
```python
import functools

import jax
import jax.numpy as jnp
from jax import lax
from jax.experimental import pallas as pl
from jax.experimental.pallas import tpu as pltpu
from jax.sharding import PartitionSpec as P

HIGHEST = lax.Precision.HIGHEST
NB = 128
SUB = 8


def dot(a, b):
    return jnp.dot(a, b, precision=HIGHEST, preferred_element_type=jnp.float32)


def dot_t(a, b):
    return lax.dot_general(
        a, b, (((0,), (0,)), ((), ())), precision=HIGHEST,
        preferred_element_type=jnp.float32,
    )


def factor_block(block, upper_ref, inverse_ref, row0, col0):
    tile = (SUB, NB)
    lane = lax.broadcasted_iota(jnp.int32, tile, 1)
    zero = jnp.zeros(tile, jnp.float32)
    groups = len(block)
    block = list(block)
    for b in range(groups):
        c0 = SUB * b
        own = block[b]
        marks = [lane == c0 + t for t in range(SUB)]
        inside = (lane >= c0) & (lane < c0 + SUB)
        after = lane >= c0 + SUB
        rows = [jnp.broadcast_to(own[s:s + 1, :], tile) for s in range(SUB)]
        d = {}
        for s in range(SUB):
            for t in range(s, SUB):
                d[s, t] = jnp.broadcast_to(rows[s][:, c0 + t:c0 + t + 1], tile)
        columns = [
            [jnp.broadcast_to(block[g][:, c0 + t:c0 + t + 1], tile) for t in range(SUB)]
            for g in range(b + 1, groups)
        ]
        v = []
        for s in range(SUB):
            unit = jnp.where(marks[s], 1.0, 0.0)
            v.append(jnp.where(inside, unit, rows[s]))
        for j in range(SUB):
            rs = lax.rsqrt(d[j, j])
            u = {k: d[j, k] * rs for k in range(j, SUB)}
            vs = v[j] * rs
            up = jnp.where(after, vs, zero)
            for k in range(j, SUB):
                up = jnp.where(marks[k], u[k], up)
            low = jnp.where(after, zero, vs)
            upper_ref[row0 + c0 + j:row0 + c0 + j + 1, col0:col0 + NB] = up[0:1, :]
            inverse_ref[row0 + c0 + j:row0 + c0 + j + 1, :] = low[0:1, :]
            for i in range(SUB):
                if i == j:
                    continue
                e = u[i] if i > j else d[i, j] * rs
                v[i] = v[i] - e * vs
                for k in range(max(j + 1, i), SUB):
                    d[i, k] = d[i, k] - e * u[k]
            v[j] = vs * rs
            for k in range(j + 1, SUB):
                d[j, k] = u[k] * rs
        for g in range(b + 1, groups):
            terms = [columns[g - b - 1][t] * v[t] for t in range(SUB)]
            while len(terms) > 1:
                terms = [terms[i] + terms[i + 1] for i in range(0, len(terms), 2)]
            block[g] = jnp.where(inside, zero, block[g]) - terms[0]


def solve_kernel(panel_ref, gram_ref, cross_ref, trailing_ref, triangle_ref, projected_ref,
                 remainder_ref, gram, cross, inverse, solved, corner, upper, lower):
    p = gram_ref.shape[0]
    blocks = p // NB
    gram[...] = gram_ref[...]
    cross[...] = cross_ref[...]
    def step(index, carry):
        start = pl.multiple_of(index * NB, NB)
        corner[...] = gram[pl.ds(start, NB), pl.ds(start, NB)]
        rows = [corner[SUB * g:SUB * (g + 1), :] for g in range(NB // SUB)]
        factor_block(rows, upper, lower, 0, 0)
        for k in range(blocks):
            pl.when(index == k)(functools.partial(update, k))
        return carry

    def update(k):
        a, z = k * NB, (k + 1) * NB
        w = lower[...]
        inverse[a:z, :] = w
        triangle_ref[a:z, a:z] = upper[...]
        if k:
            triangle_ref[a:z, 0:a] = jnp.zeros((NB, a), jnp.float32)
        if k + 1 < blocks:
            triangle_ref[a:z, z:p] = dot(w, gram[a:z, z:p])
        projected_ref[a:z, :] = dot(w, cross[a:z, :])
        for i in range(k + 1, blocks):
            lo, hi = i * NB, (i + 1) * NB
            left = triangle_ref[a:z, lo:hi]
            gram[lo:hi, lo:p] -= dot_t(left, triangle_ref[a:z, lo:p])
            cross[lo:hi, :] -= dot_t(left, projected_ref[a:z, :])

    lax.fori_loop(0, blocks, step, 0)
    for k in reversed(range(blocks)):
        a, z = k * NB, (k + 1) * NB
        rhs = projected_ref[a:z, :]
        if k + 1 < blocks:
            rhs = rhs - dot(triangle_ref[a:z, z:p], solved[z:p, :])
        solved[a:z, :] = dot_t(inverse[a:z, :], rhs)
    remainder_ref[...] = trailing_ref[...] - dot(panel_ref[...], solved[...])


def solve(panel_group, gram_sum, cross_sum, trailing):
    p = gram_sum.shape[0]
    n = cross_sum.shape[1]
    f32 = jnp.float32
    vmem = pl.BlockSpec(memory_space=pltpu.VMEM)
    return pl.pallas_call(
        solve_kernel,
        out_shape=(
            jax.ShapeDtypeStruct((p, p), f32),
            jax.ShapeDtypeStruct((p, n), f32),
            jax.ShapeDtypeStruct(trailing.shape, f32),
        ),
        in_specs=[vmem] * 4,
        out_specs=(vmem,) * 3,
        scratch_shapes=[
            pltpu.VMEM((p, p), f32),
            pltpu.VMEM((p, n), f32),
            pltpu.VMEM((p, NB), f32),
            pltpu.VMEM((p, n), f32),
            pltpu.VMEM((NB, NB), f32),
            pltpu.VMEM((NB, NB), f32),
            pltpu.VMEM((NB, NB), f32),
        ],
        name="factor_project",
    )(panel_group, gram_sum, cross_sum, trailing)


def on_device(panel_block, trailing):
    panel_group = lax.all_gather(panel_block, "dev", axis=0, tiled=True)
    gram_part = jnp.dot(panel_group.T, panel_group, precision=HIGHEST)
    cross_part = jnp.dot(panel_group.T, trailing, precision=HIGHEST)
    gram_sum, cross_sum = lax.psum((gram_part, cross_part), ("half", "grp"))
    return solve(panel_group, gram_sum, cross_sum, trailing)


def solution(mesh):
    placed = (P(("half", "grp", "dev"), None), P(("half", "grp"), "dev"))
    return jax.shard_map(
        on_device,
        mesh=mesh,
        in_specs=placed,
        out_specs=(P(), P(None, "dev"), P(("half", "grp"), "dev")),
        check_vma=False,
    )
```

time: 261 us -> 130 us (0.50)
  other arithmetic: 125 us -> 0 us
  Pallas kernels: 0 us -> 25.4 us
  local copies, waits for them, and re-layouts: 17.3 us -> 0.01 us
  matrix products: 16.6 us -> 6.95 us
  between operations: 16.9 us -> 14 us
    another operation x18 -> x0, other arithmetic: 125 us -> none  [the longest x14 83.1 us: on_device(): factor = jnp.linalg.cholesky(gram_sum)]
    pallas_call x0 -> x1, Pallas kernels: none -> 25.4 us  [solve(): pl.pallas_call(solve_kernel, out_shape=(jax.ShapeDtypeStruct((p, p), f32)...]
    another operation x17 -> x0, local copies, waits for them, and re-layouts: 11.7 us -> none
    another operation x20 -> x0, matrix products: 8.35 us -> none  [the longest x6 3.61 us: on_device(): factor = jnp.linalg.cholesky(gram_sum)]
    unnamed x19 -> x4, local copies, waits for them, and re-layouts: 3.94 us -> 0.01 us
    dot_general x3 -> x2, matrix products: 8.24 us -> 6.95 us  [the longest x1 4.44 us: on_device(): gram_part = jnp.dot(panel_group.T, panel_group, precision=HIGHEST)]
where the time goes in v1:
time: 130 us
  waiting for transfers between devices  83.9 us (65%)
  Pallas kernels  25.4 us (20%)
  between operations  14 us (11%)
  matrix products  6.95 us (5%)
    all_gather x1, waiting for transfers between devices, on_device(): panel_group = lax.all_gather(panel_block, 'dev', axis=0, tiled=True)  45.2 us
    psum x1, waiting for transfers between devices, on_device(): gram_sum, cross_sum = lax.psum((gram_part, cross_part), ('half', 'grp'))  38 us
    pallas_call x1, Pallas kernels, solve(): pl.pallas_call(solve_kernel, out_shape=(jax.ShapeDtypeStruct((p, p), f32)...  25.4 us
    dot_general x1, matrix products, on_device(): gram_part = jnp.dot(panel_group.T, panel_group, precision=HIGHEST)  4.44 us
  transfers between devices with their start and end apart: 2, of which 2 were waited for; matrix products, arithmetic and copies ran while one was open for 0% of the time, Pallas kernels for 0%

profile of v1, /device:TPU:0, one launch (start us, length us, event | category | flops | bytes accessed | tf_op | source)
XLA Modules:
  0.0 130.3 jit_solution(12805879779043711869)
XLA Ops:
  7.2 0.0 all-gather.2.cloned.1.call-start
  7.2 0.7 all-gather.2.cloned.1.call-update
  7.9 0.0 copy-start.1
  7.9 0.0 all-reduce.3.cloned.1.call-start
  8.0 45.2 %all-gather.2.cloned.1.call-done.panel_ref = f32[512,512]{1,0:T(8,128)} async-done(((f32[64,512]{1,0:T(8,128)}), f32[512,512]{1,0:T(8,128)}) %all-gather.2.cloned.1.call-update) | async-done | bytes 1048592 | tf_op jit(solution)/shard_map/all_gather | solution.py:147
  53.1 0.0 copy-start
  53.1 4.4 %fusion = f32[512,512]{1,0:T(8,128)} fusion(f32[512,512]{1,0:T(8,128)} %all-gather.2.cloned.1.call-done.panel_ref), kind=kOutput, calls=%fused_computation | convolution fusion | flops 1610612736 | bytes 2097152 | tf_op jit(solution)/shard_map/dot_general | solution.py:148
  57.6 0.0 copy-done.1
  57.6 0.0 copy-done
  57.6 2.5 %fusion.1 = f32[512,128]{1,0:T(8,128)} fusion(f32[512,512]{1,0:T(8,128)S(1)} %copy-done, f32[512,128]{1,0:T(8,128)S(1)} %copy-done.1), kind=kOutput, calls=%fused_computation.1 | convolution fusion | flops 402653184 | bytes 1572864 | tf_op jit(solution)/shard_map/dot_general | solution.py:149
  60.1 0.0 all-reduce.3.cloned.1.call-update
  60.1 38.0 %all-reduce.3.cloned.1.call-done = (f32[512,512]{1,0:T(8,128)}, f32[512,128]{1,0:T(8,128)}) async-done(((f32[512,512]{1,0:T(8,128)}, f32[512,128]{1,0:T(8,128)}), (f32[512,512]{1,0:T(8,128)}, f32[512,128]{1,0:T(8,128)})) %all-reduce.3.cloned.1.call-update) | async-done | bytes 1310736 | tf_op jit(solution)/shard_map/psum | solution.py:150
  98.1 25.4 %factor_project.1 = (f32[512,512]{1,0:T(8,128)}, f32[512,128]{1,0:T(8,128)}, f32[512,128]{1,0:T(8,128)}) custom-call(f32[512,512]{1,0:T(8,128)} %all-gather.2.cloned.1.call-done.panel_ref, f32[512,512]{1,0:T(8,128)} %get-tuple-element.3.gram_ref, f32[512,128]{1,0:T(8,128)} %get-tuple-element.4.cross_ref, f32[512,128]{1,0:T(8,128)} %trailing_ref.1), custom_call_target="tpu_custom_call" | custom-call | tf_op jit(solution)/shard_map/factor_project/pallas_call | solution.py:124
Async XLA Ops:
  7.2 46.0 %all-gather.2.cloned.1.call-start = ((), (), s32[]{:S(2)}) async-start(), calls=%async_computation | async-start | bytes 1179648 | tf_op jit(solution)/shard_map/all_gather | solution.py:147
  7.9 49.7 %copy-start.1 = (f32[512,128]{1,0:T(8,128)S(1)}, f32[512,128]{1,0:T(8,128)}, u32[]{:S(2)}) copy-start(f32[512,128]{1,0:T(8,128)} %trailing_ref.1) | copy-start | bytes 786436
  7.9 90.2 %all-reduce.3.cloned.1.call-start = ((), (), s32[]{:S(2)}) async-start(), calls=%async_computation.1 | async-start | bytes 2621440 | tf_op jit(solution)/shard_map/psum | solution.py:150
  53.1 4.5 %copy-start = (f32[512,512]{1,0:T(8,128)S(1)}, f32[512,512]{1,0:T(8,128)}, u32[]{:S(2)}) copy-start(f32[512,512]{1,0:T(8,128)} %all-gather.2.cloned.1.call-done.panel_ref) | copy-start | bytes 3145732
Sparse Core Ops, SparseCore 0:
  10.1 42.9 all-gather.1
  60.2 37.8 all-reduce.2

commit v2 on v1

--- a/solution.py
+++ b/solution.py
@@ -75,12 +75,16 @@
             block[g] = jnp.where(inside, zero, block[g]) - terms[0]
 
 
-def solve_kernel(panel_ref, gram_ref, cross_ref, trailing_ref, triangle_ref, projected_ref,
+def solve_kernel(panel_ref, packed_ref, trailing_ref, triangle_ref, projected_ref,
                  remainder_ref, gram, cross, inverse, solved, corner, upper, lower):
-    p = gram_ref.shape[0]
+    p = panel_ref.shape[1]
     blocks = p // NB
-    gram[...] = gram_ref[...]
-    cross[...] = cross_ref[...]
+    for (i, j), at in packing(p, trailing_ref.shape[1]).items():
+        part = packed_ref[at:at + NB, :]
+        if j < blocks:
+            gram[i * NB:(i + 1) * NB, j * NB:(j + 1) * NB] = part
+        else:
+            cross[i * NB:(i + 1) * NB, (j - blocks) * NB:(j - blocks + 1) * NB] = part
     def step(index, carry):
         start = pl.multiple_of(index * NB, NB)
         corner[...] = gram[pl.ds(start, NB), pl.ds(start, NB)]
@@ -116,9 +120,9 @@
     remainder_ref[...] = trailing_ref[...] - dot(panel_ref[...], solved[...])
 
 
-def solve(panel_group, gram_sum, cross_sum, trailing):
-    p = gram_sum.shape[0]
-    n = cross_sum.shape[1]
+def solve(panel_group, packed, trailing):
+    p = panel_group.shape[1]
+    n = trailing.shape[1]
     f32 = jnp.float32
     vmem = pl.BlockSpec(memory_space=pltpu.VMEM)
     return pl.pallas_call(
@@ -128,7 +132,7 @@
             jax.ShapeDtypeStruct((p, n), f32),
             jax.ShapeDtypeStruct(trailing.shape, f32),
         ),
-        in_specs=[vmem] * 4,
+        in_specs=[vmem] * 3,
         out_specs=(vmem,) * 3,
         scratch_shapes=[
             pltpu.VMEM((p, p), f32),
@@ -140,21 +144,152 @@
             pltpu.VMEM((NB, NB), f32),
         ],
         name="factor_project",
-    )(panel_group, gram_sum, cross_sum, trailing)
-
-
-def on_device(panel_block, trailing):
-    panel_group = lax.all_gather(panel_block, "dev", axis=0, tiled=True)
-    gram_part = jnp.dot(panel_group.T, panel_group, precision=HIGHEST)
-    cross_part = jnp.dot(panel_group.T, trailing, precision=HIGHEST)
-    gram_sum, cross_sum = lax.psum((gram_part, cross_part), ("half", "grp"))
-    return solve(panel_group, gram_sum, cross_sum, trailing)
+    )(panel_group, packed, trailing)
+
+
+def packing(p, n):
+    blocks = p // NB
+    where = {}
+    for i in range(blocks):
+        for j in range(i, blocks):
+            where[i, j] = len(where) * NB
+    for i in range(blocks):
+        for j in range(n // NB):
+            where[i, blocks + j] = len(where) * NB
+    return where
+
+
+def gather_kernel(halves, groups, devs, panel_ref, trailing_ref, group_ref, packed_ref, panel,
+                  total, inbox, a_send, a_recv, b_send, b_recv, r_send, r_recv):
+    mesh_ids = pl.DeviceIdType.MESH
+    mine = lax.axis_index("dev")
+    rank = lax.axis_index("half") * groups + lax.axis_index("grp")
+    pairs = devs // 2
+    pair, parity = mine // 2, mine % 2
+    levels = (halves * groups).bit_length() - 1
+    rows, p = panel_ref.shape
+    n = trailing_ref.shape[1]
+    blocks = p // NB
+
+    def slot(dev):
+        return pl.ds(pl.multiple_of(dev * rows, rows), rows)
+
+    def same(step):
+        return ((pair + step) % pairs) * 2 + parity
+
+    def at_rank(level):
+        bit = 1 << level
+        other = rank + bit * (1 - 2 * ((rank // bit) % 2))
+        return {"half": other // groups, "grp": other % groups}
+
+    beside = pair * 2 + 1 - parity
+    peers = [{"dev": same(step)} for step in range(1, pairs)] + [{"dev": beside}]
+    peers += [at_rank(level) for level in range(levels)]
+    barrier = pltpu.get_barrier_semaphore()
+    for peer in peers:
+        pl.semaphore_signal(barrier, inc=1, device_id=peer, device_id_type=mesh_ids)
+    pl.semaphore_wait(barrier, len(peers))
+
+    first = [
+        pltpu.make_async_remote_copy(
+            src_ref=panel_ref, dst_ref=panel.at[slot(mine)], send_sem=a_send.at[step],
+            recv_sem=a_recv.at[step], device_id={"dev": same(step)}, device_id_type=mesh_ids)
+        for step in range(1, pairs)
+    ]
+    onward = []
+    for step in range(pairs):
+        owner = same(pairs - step)
+        onward.append(pltpu.make_async_remote_copy(
+            src_ref=panel.at[slot(owner)] if step else panel_ref,
+            dst_ref=panel.at[slot(owner)], send_sem=b_send.at[step],
+            recv_sem=b_recv.at[step], device_id={"dev": beside}, device_id_type=mesh_ids))
+    for copy in first:
+        copy.start()
+    onward[0].start()
+    panel[slot(mine), :] = panel_ref[...]
+    for step in range(1, pairs):
+        first[step - 1].wait_recv()
+        onward[step].start()
+    for copy in onward:
+        copy.wait_recv()
+
+    where = packing(p, n)
+    for i in range(blocks):
+        left = panel[:, i * NB:(i + 1) * NB]
+        strip = dot_t(left, panel[:, i * NB:p])
+        for j in range(i, blocks):
+            at = where[i, j]
+            total[at:at + NB, :] = strip[:, (j - i) * NB:(j - i + 1) * NB]
+    crossed = dot_t(panel[...], trailing_ref[...])
+    for i in range(blocks):
+        for j in range(n // NB):
+            at = where[i, blocks + j]
+            total[at:at + NB, :] = crossed[i * NB:(i + 1) * NB, j * NB:(j + 1) * NB]
+
+    half = total.shape[0] // 2
+    low = (rank % 2) * half
+    keep = pl.ds(pl.multiple_of(low, 8), half)
+    give = pl.ds(pl.multiple_of(half - low, 8), half)
+    for level in range(levels):
+        copy = pltpu.make_async_remote_copy(
+            src_ref=total.at[keep if level else give], dst_ref=inbox.at[level],
+            send_sem=r_send.at[level], recv_sem=r_recv.at[level],
+            device_id=at_rank(level), device_id_type=mesh_ids)
+        copy.start()
+        if level == 0:
+            group_ref[...] = panel[...]
+        copy.wait()
+        total[keep, :] += inbox[level]
+    back = pltpu.make_async_remote_copy(
+        src_ref=total.at[keep], dst_ref=inbox.at[levels],
+        send_sem=r_send.at[levels], recv_sem=r_recv.at[levels],
+        device_id=at_rank(0), device_id_type=mesh_ids)
+    back.start()
+    packed_ref[keep, :] = total[keep, :]
+    for copy in first + onward:
+        copy.wait_send()
+    back.wait()
+    packed_ref[give, :] = inbox[levels]
+
+
+def gather_reduce(mesh, panel_block, trailing):
+    halves, groups, devs = (mesh.shape[name] for name in ("half", "grp", "dev"))
+    rows, p = panel_block.shape
+    n = trailing.shape[1]
+    f32 = jnp.float32
+    size = len(packing(p, n)) * NB
+    levels = (halves * groups).bit_length() - 1
+    vmem = pl.BlockSpec(memory_space=pltpu.VMEM)
+    dma = pltpu.SemaphoreType.DMA
+    return pl.pallas_call(
+        functools.partial(gather_kernel, halves, groups, devs),
+        out_shape=(
+            jax.ShapeDtypeStruct((rows * devs, p), f32),
+            jax.ShapeDtypeStruct((size, NB), f32),
+        ),
+        in_specs=[vmem] * 2,
+        out_specs=(vmem,) * 2,
+        scratch_shapes=[
+            pltpu.VMEM((rows * devs, p), f32),
+            pltpu.VMEM((size, NB), f32),
+            pltpu.VMEM((levels + 1, size // 2, NB), f32),
+            dma((devs // 2,)), dma((devs // 2,)), dma((devs // 2,)), dma((devs // 2,)),
+            dma((levels + 1,)), dma((levels + 1,)),
+        ],
+        compiler_params=pltpu.CompilerParams(collective_id=0, has_side_effects=True),
+        name="gather_reduce",
+    )(panel_block, trailing)
+
+
+def on_device(mesh, panel_block, trailing):
+    panel_group, packed = gather_reduce(mesh, panel_block, trailing)
+    return solve(panel_group, packed, trailing)
 
 
 def solution(mesh):
     placed = (P(("half", "grp", "dev"), None), P(("half", "grp"), "dev"))
     return jax.shard_map(
-        on_device,
+        functools.partial(on_device, mesh),
         mesh=mesh,
         in_specs=placed,
         out_specs=(P(), P(None, "dev"), P(("half", "grp"), "dev")),

time: 130 us -> 68.7 us (0.53)
  waiting for transfers between devices: 83.9 us -> 0 us
  Pallas kernels: 25.4 us -> 67.9 us
  between operations: 14 us -> 0.64 us
  matrix products: 6.95 us -> 0 us
    all_gather x1 -> x0, waiting for transfers between devices: 45.2 us -> none  [on_device(): panel_group = lax.all_gather(panel_block, 'dev', axis=0, tiled=True)]
    pallas_call x0 -> x1, Pallas kernels: none -> 42.7 us  [gather_reduce(): pl.pallas_call(functools.partial(gather_kernel, halves, groups, devs), ou...]
    psum x1 -> x0, waiting for transfers between devices: 38 us -> none  [on_device(): gram_sum, cross_sum = lax.psum((gram_part, cross_part), ('half', 'grp'))]
    dot_general x2 -> x0, matrix products: 6.95 us -> none  [the longest x1 4.44 us: on_device(): gram_part = jnp.dot(panel_group.T, panel_group, precision=HIGHEST)]
  transfers between devices with their start and end apart: 2 -> 0, of which waited for: 2 -> 0; matrix products, arithmetic and copies ran while one was open for 0% -> 0% of each run, Pallas kernels for 0% -> 0%
where the time goes in v2:
time: 68.7 us; the launch traced here: 68.5 us
  Pallas kernels  67.9 us (99%)
    pallas_call x1, Pallas kernels, gather_reduce(): pl.pallas_call(functools.partial(gather_kernel, halves, groups, devs), ou...  42.7 us
    pallas_call x1, Pallas kernels, solve(): pl.pallas_call(solve_kernel, out_shape=(jax.ShapeDtypeStruct((p, p), f32)...  25.2 us

profile of v2, /device:TPU:0, one launch (start us, length us, event | category | flops | bytes accessed | tf_op | source)
XLA Modules:
  0.0 68.5 jit_solution(11981074846333295825)
XLA Ops:
  0.6 42.7 %gather_reduce.1 = (f32[512,512]{1,0:T(8,128)}, f32[1792,128]{1,0:T(8,128)}) custom-call(f32[64,512]{1,0:T(8,128)} %panel_ref.1, f32[512,128]{1,0:T(8,128)} %trailing_ref.3), custom_call_target="tpu_custom_call" | custom-call | tf_op jit(solution)/shard_map/gather_reduce/pallas_call | solution.py:264
  43.3 25.2 %factor_project.1 = (f32[512,512]{1,0:T(8,128)}, f32[512,128]{1,0:T(8,128)}, f32[512,128]{1,0:T(8,128)}) custom-call(f32[512,512]{1,0:T(8,128)} %get-tuple-element.5.panel_ref, f32[1792,128]{1,0:T(8,128)} %get-tuple-element.6.packed_ref, f32[512,128]{1,0:T(8,128)} %trailing_ref.3), custom_call_target="tpu_custom_call" | custom-call | tf_op jit(solution)/shard_map/factor_project/pallas_call | solution.py:128
